TPU v7x, 256 devices: a whole 4x4x8 slice. The times are simulated.
256 devices in a mesh: tm: 32 (over z, x), region: 8 (over y, core).
Axes of the slice: x: 4, y: 4, z: 8, core: 2. Of those that a mesh axis runs over, the one named last changes fastest.
Arguments:
- start_primal: float32 [2048, 8, 3200], P('tm', 'region'), may hold values from 0 to 10, as said below
- demand: float32 [2048, 8, 3200], P('tm', 'region'), may hold values from -30 to 30
- unit_cost: float32 [8, 3200], P('region'), may hold values from -5 to 5
- build_cost: float32 [8, 128], P('region', 'tm'), may hold values from 0.5 to 2
- start_capacity: float32 [8, 128], P('region', 'tm'), may hold values from 0 to 2
- net_weights: float32 [8, 25, 3, 128, 128], P('region'), may hold values from -0.3125 to 0.3125
- net_columns: int32 [8, 25, 3], P('region'), may hold values from 0 to 24
- line_weights: float32 [8, 4, 128, 128], P('region'), may hold values from -0.25 to 0.25
- line_source: int32 [8, 4], replicated, may hold values from 0 to 7
- generator_map: int32 [8, 128], P('region'), may hold values from 0 to 127
Outputs:
- primal_final: float32 [2048, 8, 3200], P('tm', 'region')
- dual_final: float32 [2048, 8, 3200], P('tm', 'region')
- capacity_final: float32 [8, 128], P('region', 'tm')
Inputs may be any that keep to these rules, and one draw needn't show every extreme that they name: `start_primal`: Nonnegative.
All inputs are finite; a program needn't handle non-finite values.
Results may differ from a plain program's by a relative error of at most 0.0003.
Values sent between devices are 32-bit elements; how exact they have to be, the bound alone decides.
A program may use at most 64 MiB of HBM per device.

v0:
```python
import math
import jax
import jax.numpy as jnp
from jax import lax
from jax.sharding import PartitionSpec as P

ITERS = 4
HIGHEST_PRECISION = lax.Precision.HIGHEST
STEP_SCALE = 0.2
EPSILON = 1e-06


def shifted(shard, axis, by):
    devices = lax.axis_size(axis)
    pairs = [(i, i + by) for i in range(devices) if 0 <= i + by < devices]
    return lax.ppermute(shard, axis, pairs)


def network_forward(blocks, weights, columns):
    hour_count = blocks.shape[0]
    picked = jnp.take(blocks, columns.reshape(-1), axis=1)
    flat_weights = weights.reshape(-1, weights.shape[2], weights.shape[3])
    product = jnp.einsum("hpk,pkl->hpl", picked, flat_weights, precision=HIGHEST_PRECISION)
    return product.reshape(hour_count, columns.shape[0], columns.shape[1], -1).sum(axis=2)


def network_adjoint(dual_rows, weights, columns):
    hour_count = dual_rows.shape[0]
    partial_value = jnp.einsum("hil,iskl->hisk", dual_rows, weights, precision=HIGHEST_PRECISION)
    block_count = columns.shape[0]
    placing = (columns.reshape(-1)[:, None] == jnp.arange(block_count)[None, :]).astype(jnp.float32)
    stacked = partial_value.reshape(hour_count, -1, partial_value.shape[3])
    return jnp.einsum("hpk,pc->hck", stacked, placing, precision=HIGHEST_PRECISION)


def body(
    start_primal,
    demand,
    unit_cost,
    build_cost,
    start_capacity,
    net_weights,
    net_columns,
    line_weights,
    line_source,
    generator_map,
):
    hour_count, _, row_width = start_primal.shape
    block_size = net_weights.shape[3]
    block_count = row_width // block_size
    tm_count = lax.axis_size("tm")
    region_count = lax.axis_size("region")
    own_region = lax.axis_index("region")
    weights = net_weights[0]
    columns = net_columns[0]
    line_mats = line_weights[0]
    unit_rows = unit_cost.reshape(block_count, block_size)
    invest_own = start_capacity.shape[1]
    invest_all = invest_own * tm_count
    couple = 1.0 / math.sqrt(hour_count * tm_count)
    primal_count = hour_count * tm_count * region_count * row_width + region_count * invest_all
    dual_count = hour_count * tm_count * region_count * row_width
    selector = (generator_map[0][:, None] == jnp.arange(invest_all)[None, :]).astype(jnp.float32)
    line_links = (line_source[:, :, None] == jnp.arange(region_count)[None, None, :]).astype(
        jnp.float32
    )
    own_sources = lax.dynamic_index_in_dim(line_links, own_region, 0, keepdims=False)
    free_column = (jnp.arange(block_count) == 3)[None, :, None]
    free_row = (jnp.arange(block_count) < 3)[None, :, None]
    primal = start_primal.reshape(hour_count, block_count, block_size)
    target = demand.reshape(hour_count, block_count, block_size)
    dual = jnp.zeros_like(primal)
    primal_weight = jnp.float32(1.0)
    capacity, build_rows = (
        lax.all_gather(start_capacity[0], "tm", axis=0, tiled=True),
        lax.all_gather(build_cost[0], "tm", axis=0, tiled=True),
    )
    for iteration in range(ITERS):
        primal_step = STEP_SCALE / primal_weight
        dual_step = STEP_SCALE * primal_weight
        adjoint = network_adjoint(dual, weights, columns)
        after = shifted(dual[0, 0], "tm", -1)
        following = jnp.concatenate([dual[1:, 0], after[None]], axis=0)
        partial_lines = jnp.einsum(
            "hl,jkl->jhk", dual[:, 1], line_mats, precision=HIGHEST_PRECISION
        )
        line_back = lax.psum_scatter(
            jnp.einsum("jq,jhk->qhk", own_sources, partial_lines, precision=HIGHEST_PRECISION),
            "region",
            scatter_dimension=0,
            tiled=True,
        )[0]
        adjoint = adjoint.at[:, 0].add(-following).at[:, 3].add(line_back)
        column_sums = jnp.sum(dual[:, 2], axis=0)
        capacity_part = couple * jnp.dot(column_sums, selector, precision=HIGHEST_PRECISION)
        moved = primal - primal_step * (unit_rows[None] - adjoint)
        new_primal = jnp.where(free_column, moved, jnp.maximum(moved, 0.0))
        capacity_grad = lax.psum(capacity_part, "tm")
        new_capacity = jnp.maximum(capacity - primal_step * (build_rows - capacity_grad), 0.0)
        capacity_bar = 2.0 * new_capacity - capacity
        capacity_change = lax.dynamic_slice_in_dim(
            new_capacity - capacity, lax.axis_index("tm") * invest_own, invest_own, 0
        )
        primal_bar = 2.0 * new_primal - primal
        primal_local = jnp.sum((new_primal - primal) ** 2) + jnp.sum(capacity_change**2)
        if iteration + 1 < ITERS:
            primal_total = lax.psum(primal_local, ("tm", "region"))
        applied = network_forward(primal_bar, weights, columns)
        before = shifted(primal_bar[-1, 0], "tm", 1)
        earlier = jnp.concatenate([before[None], primal_bar[:-1, 0]], axis=0)
        chosen_flows = jnp.einsum(
            "jr,rhk->jhk",
            own_sources,
            lax.all_gather(primal_bar[:, 3][None], "region", axis=0, tiled=True),
            precision=HIGHEST_PRECISION,
        )
        line_flow = jnp.einsum("jhk,jkl->hl", chosen_flows, line_mats, precision=HIGHEST_PRECISION)
        picked_capacity = jnp.dot(selector, capacity_bar, precision=HIGHEST_PRECISION)
        applied = (
            applied.at[:, 0]
            .add(-earlier)
            .at[:, 1]
            .add(line_flow)
            .at[:, 2]
            .add(couple * picked_capacity[None])
        )
        moved_dual = dual + dual_step * (target - applied)
        new_dual = jnp.where(free_row, moved_dual, jnp.maximum(moved_dual, 0.0))
        if iteration + 1 < ITERS:
            dual_local = jnp.sum((new_dual - dual) ** 2)
            dual_total = lax.psum(dual_local, ("tm", "region"))
            primal_weight = jnp.sqrt(
                primal_weight
                * jnp.sqrt(primal_total / primal_count + EPSILON)
                / jnp.sqrt(dual_total / dual_count + EPSILON)
            )
        primal, dual, capacity = (new_primal, new_dual, new_capacity)
    capacity_own = lax.dynamic_slice_in_dim(
        capacity, lax.axis_index("tm") * invest_own, invest_own, 0
    )
    return (
        primal.reshape(hour_count, 1, row_width),
        dual.reshape(hour_count, 1, row_width),
        capacity_own[None],
    )


def solution(mesh):
    in_specs = (
        P("tm", "region", None),
        P("tm", "region", None),
        P("region", None),
        P("region", "tm"),
        P("region", "tm"),
        P("region", None, None, None, None),
        P("region", None, None),
        P("region", None, None, None),
        P(),
        P("region", None),
    )
    out_specs = (P("tm", "region", None), P("tm", "region", None), P("region", "tm"))
    return jax.shard_map(body, mesh=mesh, in_specs=in_specs, out_specs=out_specs, check_vma=False)
```

profile of v0, /device:TPU:1, one launch (start us, length us, event | category | flops | bytes accessed | tf_op | source)
XLA Modules:
  0.0 858.2 jit_solution(13189949462657411320)
XLA Ops:
  7.2 1.4 collective-permute-start
  9.4 1.3 convolution_bitcast_fusion.3
  12.1 0.8 copy.145
  12.9 9.0 %fusion.6 = f32[25,64,3,128]{3,1,2,0:T(8,128)S(1)} fusion(f32[1,25,3,128,128]{4,3,2,1,0:T(8,128)} %param.57), kind=kOutput, calls=%fused_computation.10 | convolution fusion | flops 943718400 | bytes 7372800 | tf_op jit(solution)/shard_map/hil,iskl->hisk/dot_general | solution.py:29
  22.0 2.4 fusion.14
  27.1 76.9 %all-reduce.6 = (f32[128]{0:T(128)S(1)}, f32[128]{0:T(128)S(1)}, f32[128]{0:T(128)S(1)}) all-reduce(f32[128]{0:T(128)S(1)} %bitcast_dynamic-update-slice_fusion.1, f32[128]{0:T(128)S(1)} %bitcast_dynamic-update-slice_fusion, f32[128]{0:T(128)S(1)} %fusion.51), channel_id=2, replica_groups=mesh['tm'=32,'region'=8] {'tm'}, use_global_device_ids=true, to_apply=%add.1 | all-reduce | flops 384 | bytes 3072 | tf_op jit(solution)/shard_map/all_gather | solution.py:75
  104.3 1.9 reduce.45
  106.3 3.1 reduce.43
  110.1 0.8 fusion.111
  110.8 1.0 fusion.60
  112.0 1.3 collective-permute-start.1
  113.3 28.2 %all-gather.2 = f32[512,1,128]{2,1,0:T(1,128)S(1)} all-gather(f32[64,1,128]{2,1,0:T(1,128)S(1)} %bitcast.385), channel_id=4, replica_groups=mesh['tm'=32,'region'=8] {'region'}, dimensions={0}, use_global_device_ids=true | all-gather | bytes 294912 | tf_op jit(solution)/shard_map/all_gather | solution.py:114
  141.5 2.1 gather_fusion
  143.6 7.9 fusion.22
  153.2 2.0 reduce_sum.150
  155.6 1.0 multiply_reduce_fusion.4
  157.0 10.5 %fusion.4 = f32[25,64,3,128]{3,1,2,0:T(8,128)} fusion(f32[1,25,3,128,128]{4,3,2,1,0:T(8,128)} %param.57, f32[64,25,128]{2,0,1:T(8,128)S(1)} %get-tuple-element.281), kind=kOutput, calls=%fused_computation.8 | convolution fusion | flops 943718400 | bytes 8192000 | tf_op jit(solution)/shard_map/hil,iskl->hisk/dot_general | solution.py:29
  167.7 55.8 %psum.73 = f32[128]{0:T(128)S(1)} all-reduce(f32[128]{0:T(128)S(1)} %fusion.49), channel_id=1, replica_groups=mesh['tm'=32,'region'=8] {'tm'}, use_global_device_ids=true, to_apply=%region_11.13 | all-reduce | flops 128 | bytes 1024 | tf_op jit(solution)/shard_map/psum | solution.py:98
  223.5 89.7 %all-reduce.5 = (f32[]{:T(128)}, f32[]{:T(128)}) all-reduce(f32[]{:T(128)S(6)} %add.249, f32[]{:T(128)} %get-tuple-element.280), channel_id=1, replica_groups=mesh['tm'=32,'region'=8] {'tm','region'}, use_global_device_ids=true, to_apply=%region_4.5 | all-reduce | flops 2 | bytes 16 | tf_op jit(solution)/shard_map/psum | solution.py:107
  314.6 1.3 collective-permute-start.2
  317.6 4.0 fusion.12
  321.8 0.8 slice.573
  322.7 1.4 copy.252
  325.8 22.6 %reduce-scatter.7.cloned.1.call-done = f32[1,64,128]{2,1,0:T(8,128)} async-done(((f32[8,64,128]{2,1,0:T(8,128)}), f32[1,64,128]{2,1,0:T(8,128)}) %reduce-scatter.7.cloned.1.call-update) | async-done | bytes 32784 | tf_op jit(solution)/shard_map/reduce_scatter | solution.py:87
  348.4 1.4 fusion.106
  349.7 2.2 multiply_reduce_fusion.3
  352.8 2.1 gather_fusion.1
  354.9 2.8 collective-permute-start.3
  357.8 16.1 %all-gather.3 = f32[512,1,128]{2,1,0:T(1,128)S(1)} all-gather(f32[64,1,128]{2,1,0:T(1,128)S(1)} %bitcast.383), channel_id=5, replica_groups=mesh['tm'=32,'region'=8] {'region'}, dimensions={0}, use_global_device_ids=true | all-gather | bytes 294912 | tf_op jit(solution)/shard_map/all_gather | solution.py:114
  373.9 7.9 fusion.20
  383.4 2.0 reduce_sum.155
  385.7 1.1 multiply_reduce_fusion.2
  387.2 10.5 %fusion.2 = f32[25,64,3,128]{3,1,2,0:T(8,128)} fusion(f32[1,25,3,128,128]{4,3,2,1,0:T(8,128)} %param.57, f32[64,25,128]{2,0,1:T(8,128)S(1)} %get-tuple-element.275), kind=kOutput, calls=%fused_computation.6 | convolution fusion | flops 943718400 | bytes 8192000 | tf_op jit(solution)/shard_map/hil,iskl->hisk/dot_general | solution.py:29
  397.9 59.1 %psum.76 = f32[128]{0:T(128)S(1)} all-reduce(f32[128]{0:T(128)S(1)} %fusion.47), channel_id=1, replica_groups=mesh['tm'=32,'region'=8] {'tm'}, use_global_device_ids=true, to_apply=%region_20.22 | all-reduce | flops 128 | bytes 1024 | tf_op jit(solution)/shard_map/psum | solution.py:98
  457.0 86.0 %all-reduce.4 = (f32[]{:T(128)}, f32[]{:T(128)}) all-reduce(f32[]{:T(128)S(6)} %add.257, f32[]{:T(128)} %get-tuple-element.274), channel_id=1, replica_groups=mesh['tm'=32,'region'=8] {'tm','region'}, use_global_device_ids=true, to_apply=%region_13.15 | all-reduce | flops 2 | bytes 16 | tf_op jit(solution)/shard_map/psum | solution.py:107
  544.5 1.3 collective-permute-start.4
  547.2 4.0 fusion.10
  551.4 0.8 slice.585
  552.2 1.4 copy.251
  555.4 23.9 %reduce-scatter.9.cloned.1.call-done = f32[1,64,128]{2,1,0:T(8,128)} async-done(((f32[8,64,128]{2,1,0:T(8,128)}), f32[1,64,128]{2,1,0:T(8,128)}) %reduce-scatter.9.cloned.1.call-update) | async-done | bytes 32784 | tf_op jit(solution)/shard_map/reduce_scatter | solution.py:87
  579.3 1.4 fusion.101
  580.7 2.2 multiply_reduce_fusion.1
  582.9 2.1 gather_fusion.2
  585.1 2.8 collective-permute-start.5
  587.9 16.1 %all-gather.4 = f32[512,1,128]{2,1,0:T(1,128)S(1)} all-gather(f32[64,1,128]{2,1,0:T(1,128)S(1)} %bitcast.384), channel_id=6, replica_groups=mesh['tm'=32,'region'=8] {'region'}, dimensions={0}, use_global_device_ids=true | all-gather | bytes 294912 | tf_op jit(solution)/shard_map/all_gather | solution.py:114
  604.0 7.9 fusion.18
  613.6 2.0 reduce_sum.160
  615.9 2.2 multiply_reduce_fusion
  618.5 10.5 %fusion = f32[25,64,3,128]{3,1,2,0:T(8,128)} fusion(f32[1,25,3,128,128]{4,3,2,1,0:T(8,128)} %param.57, f32[64,25,128]{2,0,1:T(8,128)S(1)} %get-tuple-element.271), kind=kOutput, calls=%fused_computation.4 | convolution fusion | flops 943718400 | bytes 8192000 | tf_op jit(solution)/shard_map/hil,iskl->hisk/dot_general | solution.py:29
  629.2 59.1 %psum.79 = f32[128]{0:T(128)S(1)} all-reduce(f32[128]{0:T(128)S(1)} %fusion.45), channel_id=1, replica_groups=mesh['tm'=32,'region'=8] {'tm'}, use_global_device_ids=true, to_apply=%region_29.31 | all-reduce | flops 128 | bytes 1024 | tf_op jit(solution)/shard_map/psum | solution.py:98
  688.3 86.0 %all-reduce.3 = (f32[]{:T(128)}, f32[]{:T(128)}) all-reduce(f32[]{:T(128)S(6)} %add.266, f32[]{:T(128)} %get-tuple-element.270), channel_id=1, replica_groups=mesh['tm'=32,'region'=8] {'tm','region'}, use_global_device_ids=true, to_apply=%region_22.24 | all-reduce | flops 2 | bytes 16 | tf_op jit(solution)/shard_map/psum | solution.py:107
  775.8 1.5 collective-permute-start.6
  778.5 4.0 fusion.8
  784.1 1.4 copy.250
  786.6 24.2 %reduce-scatter.11.cloned.1.call-done = f32[1,64,128]{2,1,0:T(8,128)} async-done(((f32[8,64,128]{2,1,0:T(8,128)}), f32[1,64,128]{2,1,0:T(8,128)}) %reduce-scatter.11.cloned.1.call-update) | async-done | bytes 32784 | tf_op jit(solution)/shard_map/reduce_scatter | solution.py:87
  810.8 1.4 fusion.96
  812.2 2.7 multiply_subtract_fusion
  814.9 2.2 gather_fusion.3
  817.0 2.8 collective-permute-start.7
  819.9 16.1 %all-gather.5 = f32[512,1,128]{2,1,0:T(1,128)S(1)} all-gather(f32[64,1,128]{2,1,0:T(1,128)S(1)} %bitcast.382), channel_id=7, replica_groups=mesh['tm'=32,'region'=8] {'region'}, dimensions={0}, use_global_device_ids=true | all-gather | bytes 294912 | tf_op jit(solution)/shard_map/all_gather | solution.py:114
  836.0 8.0 fusion.16
  844.9 1.7 reshape.912
  846.6 2.0 reduce_sum.162
  849.6 1.7 reshape.913
  (142 shorter events, 22.9 us)
Async XLA Ops:
  7.2 97.1 %copy-start = (f32[64,1,3200]{2,1,0:T(1,128)S(1)}, f32[64,1,3200]{2,1,0:T(1,128)}, u32[]{:S(2)}) copy-start(f32[64,1,3200]{2,1,0:T(1,128)} %param.53) | copy-start | bytes 2457604
  7.2 102.9 %reduce-scatter.5.cloned.1.call-start = ((), (), s32[]{:S(2)}) async-start(), calls=%async_computation.4 | async-start | bytes 294912 | tf_op jit(solution)/shard_map/reduce_scatter | solution.py:87
  7.2 102.8 %collective-permute-start = (f32[128]{0:T(128)S(1)}, f32[128]{0:T(128)S(1)}, u32[]{:S(2)}, u32[]{:S(2)}) collective-permute-start(f32[128]{0:T(128)S(1)} %broadcast.305), channel_id=1, source_target_pairs={{8,0},{16,8},{24,16},{32,24},{40,32},{48,40},{56,48},{64,56},{72,6... | collective-permute-start | bytes 1544 | tf_op jit(solution)/shard_map/ppermute | solution.py:16
  12.0 336.4 %reduce-scatter.7.cloned.1.call-start = ((), (), s32[]{:S(2)}) async-start(), calls=%async_computation.5 | async-start | bytes 294912 | tf_op jit(solution)/shard_map/reduce_scatter | solution.py:87
  24.4 1.0 copy-start.14
  24.4 1.3 copy-start.16
  24.4 2.5 copy-start.12
  24.4 2.6 copy-start.13
  24.4 79.8 %copy-start.11 = (f32[1,3200]{1,0:T(1,128)S(1)}, f32[1,3200]{1,0:T(1,128)}, u32[]{:S(2)}) copy-start(f32[1,3200]{1,0:T(1,128)} %param.54) | copy-start | bytes 38404
  112.0 43.3 %collective-permute-start.1 = (f32[128]{0:T(128)S(1)}, f32[128]{0:T(128)S(1)}, u32[]{:S(2)}, u32[]{:S(2)}) collective-permute-start(f32[128]{0:T(128)S(1)} %slice_bitcast_fusion.16), channel_id=1, source_target_pairs={{0,8},{8,16},{16,24},{24,32},{32,40},{40,48},{48,56},{56,64},{64,7... | collective-permute-start | bytes 1544 | tf_op jit(solution)/shard_map/ppermute | solution.py:16
  151.5 3.8 copy-start.2
  156.6 10.9 %copy-start.8 = (f32[64,25,128]{2,0,1:T(8,128)}, f32[64,25,128]{2,0,1:T(8,128)S(1)}, u32[]{:S(2)}) copy-start(f32[64,25,128]{2,0,1:T(8,128)S(1)} %get-tuple-element.281) | copy-start | bytes 2457604
  167.7 153.9 %copy-start.15 = (s32[1,128]{1,0:T(1,128)S(1)}, s32[1,128]{1,0:T(1,128)}, u32[]{:S(2)}) copy-start(s32[1,128]{1,0:T(1,128)} %param.61) | copy-start | bytes 1540
  314.6 10.5 %collective-permute-start.2 = (f32[128]{0:T(128)S(1)}, f32[128]{0:T(128)S(1)}, u32[]{:S(2)}, u32[]{:S(2)}) collective-permute-start(f32[128]{0:T(128)S(1)} %slice_bitcast_fusion.15), channel_id=1, source_target_pairs={{8,0},{16,8},{24,16},{32,24},{40,32},{48,40},{56,48},{64,56},{72,6... | collective-permute-start | bytes 1544 | tf_op jit(solution)/shard_map/ppermute | solution.py:16
  317.1 262.2 %reduce-scatter.9.cloned.1.call-start = ((), (), s32[]{:S(2)}) async-start(), calls=%async_computation.6 | async-start | bytes 294912 | tf_op jit(solution)/shard_map/reduce_scatter | solution.py:87
  351.9 0.9 copy-start.3
  354.9 30.4 %collective-permute-start.3 = (f32[128]{0:T(128)S(1)}, f32[128]{0:T(128)S(1)}, u32[]{:S(2)}, u32[]{:S(2)}) collective-permute-start(f32[128]{0:T(128)S(1)} %slice_bitcast_fusion.14), channel_id=1, source_target_pairs={{0,8},{8,16},{16,24},{24,32},{32,40},{40,48},{48,56},{56,64},{64,7... | collective-permute-start | bytes 1544 | tf_op jit(solution)/shard_map/ppermute | solution.py:16
  381.8 4.0 copy-start.9
  386.8 10.9 %copy-start.7 = (f32[64,25,128]{2,0,1:T(8,128)}, f32[64,25,128]{2,0,1:T(8,128)S(1)}, u32[]{:S(2)}) copy-start(f32[64,25,128]{2,0,1:T(8,128)S(1)} %get-tuple-element.275) | copy-start | bytes 2457604
  544.5 10.3 %collective-permute-start.4 = (f32[128]{0:T(128)S(1)}, f32[128]{0:T(128)S(1)}, u32[]{:S(2)}, u32[]{:S(2)}) collective-permute-start(f32[128]{0:T(128)S(1)} %slice_bitcast_fusion.13), channel_id=1, source_target_pairs={{8,0},{16,8},{24,16},{32,24},{40,32},{48,40},{56,48},{64,56},{72,6... | collective-permute-start | bytes 1544 | tf_op jit(solution)/shard_map/ppermute | solution.py:16
  547.0 263.9 %reduce-scatter.11.cloned.1.call-start = ((), (), s32[]{:S(2)}) async-start(), calls=%async_computation.7 | async-start | bytes 294912 | tf_op jit(solution)/shard_map/reduce_scatter | solution.py:87
  551.2 29.5 %copy-start.4 = (f32[64,25,128]{2,0,1:T(8,128)S(1)}, f32[64,25,128]{2,0,1:T(8,128)}, u32[]{:S(2)}) copy-start(f32[64,25,128]{2,0,1:T(8,128)} %copy-done.3) | copy-start | bytes 2457604
  585.1 30.5 %collective-permute-start.5 = (f32[128]{0:T(128)S(1)}, f32[128]{0:T(128)S(1)}, u32[]{:S(2)}, u32[]{:S(2)}) collective-permute-start(f32[128]{0:T(128)S(1)} %slice_bitcast_fusion.12), channel_id=1, source_target_pairs={{0,8},{8,16},{16,24},{24,32},{32,40},{40,48},{48,56},{56,64},{64,7... | collective-permute-start | bytes 1544 | tf_op jit(solution)/shard_map/ppermute | solution.py:16
  618.1 10.9 %copy-start.5 = (f32[64,25,128]{2,0,1:T(8,128)}, f32[64,25,128]{2,0,1:T(8,128)S(1)}, u32[]{:S(2)}) copy-start(f32[64,25,128]{2,0,1:T(8,128)S(1)} %get-tuple-element.271) | copy-start | bytes 2457604
  775.8 10.2 %collective-permute-start.6 = (f32[128]{0:T(128)S(1)}, f32[128]{0:T(128)S(1)}, u32[]{:S(2)}, u32[]{:S(2)}) collective-permute-start(f32[128]{0:T(128)S(1)} %slice_bitcast_fusion.11), channel_id=1, source_target_pairs={{8,0},{16,8},{24,16},{32,24},{40,32},{48,40},{56,48},{64,56},{72,6... | collective-permute-start | bytes 1544 | tf_op jit(solution)/shard_map/ppermute | solution.py:16
  817.0 31.6 %collective-permute-start.7 = (f32[128]{0:T(128)S(1)}, f32[128]{0:T(128)S(1)}, u32[]{:S(2)}, u32[]{:S(2)}) collective-permute-start(f32[128]{0:T(128)S(1)} %slice_bitcast_fusion.10), channel_id=1, source_target_pairs={{0,8},{8,16},{16,24},{24,32},{32,40},{40,48},{48,56},{56,64},{64,7... | collective-permute-start | bytes 1544 | tf_op jit(solution)/shard_map/ppermute | solution.py:16
  836.0 8.4 copy-start.10
  844.9 4.1 copy-start.6
  848.9 2.4 copy-start.1
Sparse Core Ops, SparseCore 0:
  12.1 36.2 reduce-scatter.4
  317.2 31.0 reduce-scatter.6
  547.1 32.1 reduce-scatter.8
  778.6 32.1 reduce-scatter.10
where the time goes:
time: 867 us; the launch traced here: 858 us
  blocking collectives  589 us (68%)
  matrix products  94.9 us (11%)
  waiting for transfers between devices  70.8 us (8%)
  other arithmetic  35 us (4%)
  local copies, waits for them, and re-layouts  28.8 us (3%)
  between operations  23.7 us (3%)
  starting transfers between devices  16 us (2%)
    psum x3, blocking collectives, body(): primal_total = lax.psum(primal_local, ('tm', 'region'))  262 us
    psum x3, blocking collectives, body(): capacity_grad = lax.psum(capacity_part, 'tm')  174 us
    all_gather x1, blocking collectives, body(): lax.all_gather(start_capacity[0], 'tm', axis=0, tiled=True)  76.9 us
    all_gather x4, blocking collectives, body(): lax.all_gather(primal_bar[:, 3][None], 'region', axis=0, tiled=True)  76.5 us
    reduce_scatter x4, waiting for transfers between devices, body(): lax.psum_scatter(jnp.einsum('jq,jhk->qhk', own_sources, partial_lines, pr...  70.7 us
    dot_general x4, matrix products, network_adjoint(): jnp.einsum('hil,iskl->hisk', dual_rows, weights, precision=HIGHEST_PRECIS...  40.4 us
    dot_general x4, matrix products, network_forward(): jnp.einsum('hpk,pkl->hpl', picked, flat_weights, precision=HIGHEST_PRECIS...  31.7 us
  transfers between devices with their start and end apart: 12, of which 3 were waited for; matrix products, arithmetic and copies ran while one was open for 11% of the time, Pallas kernels for 0%

commit v1 on v0

--- a/solution.py
+++ b/solution.py
@@ -111,7 +111,12 @@
         chosen_flows = jnp.einsum(
             "jr,rhk->jhk",
             own_sources,
-            lax.all_gather(primal_bar[:, 3][None], "region", axis=0, tiled=True),
+            jnp.concatenate(
+                lax.all_to_all(
+                    jnp.stack(lax.axis_size("region") * [primal_bar[:, 3][None]]), "region", 0, 0
+                ),
+                axis=0,
+            ),
             precision=HIGHEST_PRECISION,
         )
         line_flow = jnp.einsum("jhk,jkl->hl", chosen_flows, line_mats, precision=HIGHEST_PRECISION)

time: 867 us -> 844 us (0.973)
  blocking collectives: 589 us -> 519 us
  starting transfers between devices: 16 us -> 55.5 us
    all_gather x4 -> x0, blocking collectives: 76.5 us -> none  [body(): lax.all_gather(primal_bar[:, 3][None], 'region', axis=0, tiled=True)]
    all_to_all x0 -> x4, starting transfers between devices: none -> 39.7 us  [body(): lax.all_to_all(jnp.stack(lax.axis_size('region') * [primal_bar[:, 3][None...]
  transfers between devices with their start and end apart: 12 -> 16, of which waited for: 3 -> 3; matrix products, arithmetic and copies ran while one was open for 11% -> 12% of each run, Pallas kernels for 0% -> 0%
where the time goes in v1:
time: 844 us; the launch traced here: 835 us
  blocking collectives  519 us (61%)
  matrix products  96.3 us (11%)
  waiting for transfers between devices  69.7 us (8%)
  starting transfers between devices  55.5 us (7%)
  other arithmetic  38.7 us (5%)
  local copies, waits for them, and re-layouts  31.8 us (4%)
  between operations  23.7 us (3%)
    psum x3, blocking collectives, body(): primal_total = lax.psum(primal_local, ('tm', 'region'))  269 us
    psum x3, blocking collectives, body(): capacity_grad = lax.psum(capacity_part, 'tm')  174 us
    all_gather x1, blocking collectives, body(): lax.all_gather(start_capacity[0], 'tm', axis=0, tiled=True)  76.4 us
    reduce_scatter x4, waiting for transfers between devices, body(): lax.psum_scatter(jnp.einsum('jq,jhk->qhk', own_sources, partial_lines, pr...  69.6 us
    dot_general x4, matrix products, network_adjoint(): jnp.einsum('hil,iskl->hisk', dual_rows, weights, precision=HIGHEST_PRECIS...  40.4 us
    all_to_all x4, starting transfers between devices, body(): lax.all_to_all(jnp.stack(lax.axis_size('region') * [primal_bar[:, 3][None...  39.7 us
    dot_general x4, matrix products, network_forward(): jnp.einsum('hpk,pkl->hpl', picked, flat_weights, precision=HIGHEST_PRECIS...  31.7 us
  transfers between devices with their start and end apart: 16, of which 3 were waited for; matrix products, arithmetic and copies ran while one was open for 12% of the time, Pallas kernels for 0%

profile of v1, /device:TPU:1, one launch (start us, length us, event | category | flops | bytes accessed | tf_op | source)
XLA Modules:
  0.0 834.7 jit_solution(5229903335786133426)
XLA Ops:
  7.2 1.4 collective-permute-start
  9.4 1.3 convolution_bitcast_fusion.3
  12.9 9.0 %fusion.6 = f32[25,64,3,128]{3,1,2,0:T(8,128)S(1)} fusion(f32[1,25,3,128,128]{4,3,2,1,0:T(8,128)} %param.57), kind=kOutput, calls=%fused_computation.10 | convolution fusion | flops 943718400 | bytes 7372800 | tf_op jit(solution)/shard_map/hil,iskl->hisk/dot_general | solution.py:29
  21.9 2.4 fusion.14
  27.1 76.4 %all-reduce.6 = (f32[128]{0:T(128)S(1)}, f32[128]{0:T(128)S(1)}, f32[128]{0:T(128)S(1)}) all-reduce(f32[128]{0:T(128)S(1)} %bitcast_dynamic-update-slice_fusion.1, f32[128]{0:T(128)S(1)} %bitcast_dynamic-update-slice_fusion, f32[128]{0:T(128)S(1)} %fusion.51), channel_id=2, replica_groups=mesh['tm'=32,'region'=8] {'tm'}, use_global_device_ids=true, to_apply=%add.1 | all-reduce | flops 384 | bytes 3072 | tf_op jit(solution)/shard_map/all_gather | solution.py:75
  103.8 1.9 reduce.45
  105.8 3.1 reduce.43
  110.3 1.0 fusion.60
  111.5 1.3 collective-permute-start.1
  113.5 19.5 %all-to-all-start = ((f32[8,1,64,128]{3,2,1,0:T(8,128)}), f32[8,1,64,128]{3,2,1,0:T(8,128)S(1)}, u32[]{:S(2)}, u32[]{:S(2)}) async-start(f32[8,1,64,128]{3,2,1,0:T(8,128)} %stack.12), calls=%async_computation.1 | async-start | bytes 524288 | tf_op jit(solution)/shard_map/all_to_all | solution.py:115
  133.0 2.1 gather_fusion
  135.1 7.9 fusion.22
  144.4 2.0 reduce_sum.150
  147.2 1.0 multiply_reduce_fusion.4
  148.6 10.5 %fusion.4 = f32[25,64,3,128]{3,1,2,0:T(8,128)} fusion(f32[1,25,3,128,128]{4,3,2,1,0:T(8,128)} %param.57, f32[64,25,128]{2,0,1:T(8,128)S(1)} %get-tuple-element.281), kind=kOutput, calls=%fused_computation.8 | convolution fusion | flops 943718400 | bytes 8192000 | tf_op jit(solution)/shard_map/hil,iskl->hisk/dot_general | solution.py:29
  159.3 55.7 %psum.73 = f32[128]{0:T(128)S(1)} all-reduce(f32[128]{0:T(128)S(1)} %fusion.49), channel_id=1, replica_groups=mesh['tm'=32,'region'=8] {'tm'}, use_global_device_ids=true, to_apply=%region_11.13 | all-reduce | flops 128 | bytes 1024 | tf_op jit(solution)/shard_map/psum | solution.py:98
  215.0 90.3 %all-reduce.5 = (f32[]{:T(128)}, f32[]{:T(128)}) all-reduce(f32[]{:T(128)S(6)} %add.249, f32[]{:T(128)} %get-tuple-element.280), channel_id=1, replica_groups=mesh['tm'=32,'region'=8] {'tm','region'}, use_global_device_ids=true, to_apply=%region_4.5 | all-reduce | flops 2 | bytes 16 | tf_op jit(solution)/shard_map/psum | solution.py:107
  306.7 1.7 collective-permute-start.2
  309.6 4.0 fusion.12
  313.9 0.8 slice.573
  314.7 1.4 copy.256
  317.9 23.1 %reduce-scatter.7.cloned.1.call-done = f32[1,64,128]{2,1,0:T(8,128)} async-done(((f32[8,64,128]{2,1,0:T(8,128)}), f32[1,64,128]{2,1,0:T(8,128)}) %reduce-scatter.7.cloned.1.call-update) | async-done | bytes 32784 | tf_op jit(solution)/shard_map/reduce_scatter | solution.py:87
  341.0 1.4 fusion.110
  342.4 2.2 multiply_reduce_fusion.3
  345.5 2.1 gather_fusion.1
  347.6 2.8 collective-permute-start.3
  351.1 6.8 all-to-all-start.1
  357.9 7.9 fusion.20
  367.2 2.0 reduce_sum.155
  370.0 1.1 multiply_reduce_fusion.2
  371.4 10.5 %fusion.2 = f32[25,64,3,128]{3,1,2,0:T(8,128)} fusion(f32[1,25,3,128,128]{4,3,2,1,0:T(8,128)} %param.57, f32[64,25,128]{2,0,1:T(8,128)S(1)} %get-tuple-element.275), kind=kOutput, calls=%fused_computation.6 | convolution fusion | flops 943718400 | bytes 8192000 | tf_op jit(solution)/shard_map/hil,iskl->hisk/dot_general | solution.py:29
  382.1 59.1 %psum.76 = f32[128]{0:T(128)S(1)} all-reduce(f32[128]{0:T(128)S(1)} %fusion.47), channel_id=1, replica_groups=mesh['tm'=32,'region'=8] {'tm'}, use_global_device_ids=true, to_apply=%region_20.22 | all-reduce | flops 128 | bytes 1024 | tf_op jit(solution)/shard_map/psum | solution.py:98
  441.2 89.2 %all-reduce.4 = (f32[]{:T(128)}, f32[]{:T(128)}) all-reduce(f32[]{:T(128)S(6)} %add.257, f32[]{:T(128)} %get-tuple-element.274), channel_id=1, replica_groups=mesh['tm'=32,'region'=8] {'tm','region'}, use_global_device_ids=true, to_apply=%region_13.15 | all-reduce | flops 2 | bytes 16 | tf_op jit(solution)/shard_map/psum | solution.py:107
  531.8 1.5 collective-permute-start.4
  534.5 4.0 fusion.10
  539.6 1.4 copy.255
  542.7 23.2 %reduce-scatter.9.cloned.1.call-done = f32[1,64,128]{2,1,0:T(8,128)} async-done(((f32[8,64,128]{2,1,0:T(8,128)}), f32[1,64,128]{2,1,0:T(8,128)}) %reduce-scatter.9.cloned.1.call-update) | async-done | bytes 32784 | tf_op jit(solution)/shard_map/reduce_scatter | solution.py:87
  565.9 1.4 fusion.105
  567.3 2.2 multiply_reduce_fusion.1
  569.5 2.1 gather_fusion.2
  571.7 2.8 collective-permute-start.5
  575.2 6.7 all-to-all-start.2
  582.0 7.9 fusion.18
  591.2 2.9 reduce_sum.160
  594.1 1.4 fusion.104
  595.9 1.7 fusion.39
  597.6 1.4 fusion.103
  599.0 2.2 multiply_reduce_fusion
  601.5 10.5 %fusion = f32[25,64,3,128]{3,1,2,0:T(8,128)} fusion(f32[1,25,3,128,128]{4,3,2,1,0:T(8,128)} %param.57, f32[64,25,128]{2,0,1:T(8,128)S(1)} %get-tuple-element.271), kind=kOutput, calls=%fused_computation.4 | convolution fusion | flops 943718400 | bytes 8192000 | tf_op jit(solution)/shard_map/hil,iskl->hisk/dot_general | solution.py:29
  612.2 59.1 %psum.79 = f32[128]{0:T(128)S(1)} all-reduce(f32[128]{0:T(128)S(1)} %fusion.45), channel_id=1, replica_groups=mesh['tm'=32,'region'=8] {'tm'}, use_global_device_ids=true, to_apply=%region_29.31 | all-reduce | flops 128 | bytes 1024 | tf_op jit(solution)/shard_map/psum | solution.py:98
  671.3 89.2 %all-reduce.3 = (f32[]{:T(128)}, f32[]{:T(128)}) all-reduce(f32[]{:T(128)S(6)} %add.266, f32[]{:T(128)} %get-tuple-element.270), channel_id=1, replica_groups=mesh['tm'=32,'region'=8] {'tm','region'}, use_global_device_ids=true, to_apply=%region_22.24 | all-reduce | flops 2 | bytes 16 | tf_op jit(solution)/shard_map/psum | solution.py:107
  761.9 1.5 collective-permute-start.6
  764.6 4.0 fusion.8
  770.3 1.4 copy.254
  772.8 23.3 %reduce-scatter.11.cloned.1.call-done = f32[1,64,128]{2,1,0:T(8,128)} async-done(((f32[8,64,128]{2,1,0:T(8,128)}), f32[1,64,128]{2,1,0:T(8,128)}) %reduce-scatter.11.cloned.1.call-update) | async-done | bytes 32784 | tf_op jit(solution)/shard_map/reduce_scatter | solution.py:87
  796.1 1.4 fusion.100
  797.4 2.7 multiply_subtract_fusion
  800.1 2.2 gather_fusion.3
  802.3 2.8 collective-permute-start.7
  805.8 6.7 all-to-all-start.3
  812.5 8.0 fusion.16
  821.0 1.7 reshape.940
  822.7 2.1 reduce_sum.162
  826.3 1.7 reshape.941
  (152 shorter events, 27.2 us)
Async XLA Ops:
  7.2 96.6 %copy-start = (f32[64,1,3200]{2,1,0:T(1,128)S(1)}, f32[64,1,3200]{2,1,0:T(1,128)}, u32[]{:S(2)}) copy-start(f32[64,1,3200]{2,1,0:T(1,128)} %param.53) | copy-start | bytes 2457604
  7.2 102.4 %reduce-scatter.5.cloned.1.call-start = ((), (), s32[]{:S(2)}) async-start(), calls=%async_computation.8 | async-start | bytes 294912 | tf_op jit(solution)/shard_map/reduce_scatter | solution.py:87
  7.2 102.3 %collective-permute-start = (f32[128]{0:T(128)S(1)}, f32[128]{0:T(128)S(1)}, u32[]{:S(2)}, u32[]{:S(2)}) collective-permute-start(f32[128]{0:T(128)S(1)} %broadcast.313), channel_id=1, source_target_pairs={{8,0},{16,8},{24,16},{32,24},{40,32},{48,40},{56,48},{64,56},{72,6... | collective-permute-start | bytes 1544 | tf_op jit(solution)/shard_map/ppermute | solution.py:16
  24.3 1.0 copy-start.15
  24.3 1.3 copy-start.17
  24.4 2.5 copy-start.13
  24.4 2.6 copy-start.14
  24.4 79.3 %copy-start.12 = (f32[1,3200]{1,0:T(1,128)S(1)}, f32[1,3200]{1,0:T(1,128)}, u32[]{:S(2)}) copy-start(f32[1,3200]{1,0:T(1,128)} %param.54) | copy-start | bytes 38404
  111.5 34.9 %collective-permute-start.1 = (f32[128]{0:T(128)S(1)}, f32[128]{0:T(128)S(1)}, u32[]{:S(2)}, u32[]{:S(2)}) collective-permute-start(f32[128]{0:T(128)S(1)} %slice_bitcast_fusion.20), channel_id=1, source_target_pairs={{0,8},{8,16},{16,24},{24,32},{32,40},{40,48},{48,56},{56,64},{64,7... | collective-permute-start | bytes 1544 | tf_op jit(solution)/shard_map/ppermute | solution.py:16
  113.5 32.9 %all-to-all-start = ((f32[8,1,64,128]{3,2,1,0:T(8,128)}), f32[8,1,64,128]{3,2,1,0:T(8,128)S(1)}, u32[]{:S(2)}, u32[]{:S(2)}) async-start(f32[8,1,64,128]{3,2,1,0:T(8,128)} %stack.12), calls=%async_computation.1 | async-start | bytes 524288 | tf_op jit(solution)/shard_map/all_to_all | solution.py:115
  133.0 208.0 %reduce-scatter.7.cloned.1.call-start = ((), (), s32[]{:S(2)}) async-start(), calls=%async_computation.9 | async-start | bytes 294912 | tf_op jit(solution)/shard_map/reduce_scatter | solution.py:87
  143.0 3.8 copy-start.2
  148.2 10.9 %copy-start.9 = (f32[64,25,128]{2,0,1:T(8,128)}, f32[64,25,128]{2,0,1:T(8,128)S(1)}, u32[]{:S(2)}) copy-start(f32[64,25,128]{2,0,1:T(8,128)S(1)} %get-tuple-element.281) | copy-start | bytes 2457604
  159.3 154.4 %copy-start.16 = (s32[1,128]{1,0:T(1,128)S(1)}, s32[1,128]{1,0:T(1,128)}, u32[]{:S(2)}) copy-start(s32[1,128]{1,0:T(1,128)} %param.61) | copy-start | bytes 1540
  306.7 10.6 %collective-permute-start.2 = (f32[128]{0:T(128)S(1)}, f32[128]{0:T(128)S(1)}, u32[]{:S(2)}, u32[]{:S(2)}) collective-permute-start(f32[128]{0:T(128)S(1)} %slice_bitcast_fusion.19), channel_id=1, source_target_pairs={{8,0},{16,8},{24,16},{32,24},{40,32},{48,40},{56,48},{64,56},{72,6... | collective-permute-start | bytes 1544 | tf_op jit(solution)/shard_map/ppermute | solution.py:16
  344.6 0.9 copy-start.3
  347.6 21.6 %collective-permute-start.3 = (f32[128]{0:T(128)S(1)}, f32[128]{0:T(128)S(1)}, u32[]{:S(2)}, u32[]{:S(2)}) collective-permute-start(f32[128]{0:T(128)S(1)} %slice_bitcast_fusion.18), channel_id=1, source_target_pairs={{0,8},{8,16},{16,24},{24,32},{32,40},{40,48},{48,56},{56,64},{64,7... | collective-permute-start | bytes 1544 | tf_op jit(solution)/shard_map/ppermute | solution.py:16
  351.1 18.1 %all-to-all-start.1 = ((f32[8,1,64,128]{3,2,1,0:T(8,128)}), f32[8,1,64,128]{3,2,1,0:T(8,128)S(1)}, u32[]{:S(2)}, u32[]{:S(2)}) async-start(f32[8,1,64,128]{3,2,1,0:T(8,128)} %stack.13), calls=%async_computation.3 | async-start | bytes 524288 | tf_op jit(solution)/shard_map/all_to_all | solution.py:115
  357.9 208.0 %reduce-scatter.9.cloned.1.call-start = ((), (), s32[]{:S(2)}) async-start(), calls=%async_computation.10 | async-start | bytes 294912 | tf_op jit(solution)/shard_map/reduce_scatter | solution.py:87
  365.8 4.1 copy-start.10
  371.0 10.9 %copy-start.7 = (f32[64,25,128]{2,0,1:T(8,128)}, f32[64,25,128]{2,0,1:T(8,128)S(1)}, u32[]{:S(2)}) copy-start(f32[64,25,128]{2,0,1:T(8,128)S(1)} %get-tuple-element.275) | copy-start | bytes 2457604
  531.8 10.3 %collective-permute-start.4 = (f32[128]{0:T(128)S(1)}, f32[128]{0:T(128)S(1)}, u32[]{:S(2)}, u32[]{:S(2)}) collective-permute-start(f32[128]{0:T(128)S(1)} %slice_bitcast_fusion.17), channel_id=1, source_target_pairs={{8,0},{16,8},{24,16},{32,24},{40,32},{48,40},{56,48},{64,56},{72,6... | collective-permute-start | bytes 1544 | tf_op jit(solution)/shard_map/ppermute | solution.py:16
  538.5 28.8 %copy-start.4 = (f32[64,25,128]{2,0,1:T(8,128)S(1)}, f32[64,25,128]{2,0,1:T(8,128)}, u32[]{:S(2)}) copy-start(f32[64,25,128]{2,0,1:T(8,128)} %copy-done.3) | copy-start | bytes 2457604
  571.7 22.5 %collective-permute-start.5 = (f32[128]{0:T(128)S(1)}, f32[128]{0:T(128)S(1)}, u32[]{:S(2)}, u32[]{:S(2)}) collective-permute-start(f32[128]{0:T(128)S(1)} %slice_bitcast_fusion.16), channel_id=1, source_target_pairs={{0,8},{8,16},{16,24},{24,32},{32,40},{40,48},{48,56},{56,64},{64,7... | collective-permute-start | bytes 1544 | tf_op jit(solution)/shard_map/ppermute | solution.py:16
  575.2 20.3 %all-to-all-start.2 = ((f32[8,1,64,128]{3,2,1,0:T(8,128)}), f32[8,1,64,128]{3,2,1,0:T(8,128)S(1)}, u32[]{:S(2)}, u32[]{:S(2)}) async-start(f32[8,1,64,128]{3,2,1,0:T(8,128)} %stack.14), calls=%async_computation.5 | async-start | bytes 524288 | tf_op jit(solution)/shard_map/all_to_all | solution.py:115
  582.0 214.1 %reduce-scatter.11.cloned.1.call-start = ((), (), s32[]{:S(2)}) async-start(), calls=%async_computation.11 | async-start | bytes 294912 | tf_op jit(solution)/shard_map/reduce_scatter | solution.py:87
  589.9 9.1 %copy-start.8 = (f32[64,25,128]{2,0,1:T(8,128)S(1)}, f32[64,25,128]{2,0,1:T(8,128)}, u32[]{:S(2)}) copy-start(f32[64,25,128]{2,0,1:T(8,128)} %copy-done.7) | copy-start | bytes 2457604
  601.1 10.9 %copy-start.5 = (f32[64,25,128]{2,0,1:T(8,128)}, f32[64,25,128]{2,0,1:T(8,128)S(1)}, u32[]{:S(2)}) copy-start(f32[64,25,128]{2,0,1:T(8,128)S(1)} %get-tuple-element.271) | copy-start | bytes 2457604
  761.9 10.2 %collective-permute-start.6 = (f32[128]{0:T(128)S(1)}, f32[128]{0:T(128)S(1)}, u32[]{:S(2)}, u32[]{:S(2)}) collective-permute-start(f32[128]{0:T(128)S(1)} %slice_bitcast_fusion.15), channel_id=1, source_target_pairs={{8,0},{16,8},{24,16},{32,24},{40,32},{48,40},{56,48},{64,56},{72,6... | collective-permute-start | bytes 1544 | tf_op jit(solution)/shard_map/ppermute | solution.py:16
  802.3 22.6 %collective-permute-start.7 = (f32[128]{0:T(128)S(1)}, f32[128]{0:T(128)S(1)}, u32[]{:S(2)}, u32[]{:S(2)}) collective-permute-start(f32[128]{0:T(128)S(1)} %slice_bitcast_fusion.14), channel_id=1, source_target_pairs={{0,8},{8,16},{16,24},{24,32},{32,40},{40,48},{48,56},{56,64},{64,7... | collective-permute-start | bytes 1544 | tf_op jit(solution)/shard_map/ppermute | solution.py:16
  805.8 19.0 %all-to-all-start.3 = ((f32[8,1,64,128]{3,2,1,0:T(8,128)}), f32[8,1,64,128]{3,2,1,0:T(8,128)S(1)}, u32[]{:S(2)}, u32[]{:S(2)}) async-start(f32[8,1,64,128]{3,2,1,0:T(8,128)} %stack.15), calls=%async_computation.7 | async-start | bytes 524288 | tf_op jit(solution)/shard_map/all_to_all | solution.py:115
  812.5 8.0 copy-start.11
  822.7 2.8 copy-start.6
  825.6 2.4 copy-start.1
Sparse Core Ops, SparseCore 0:
  12.1 36.2 reduce-scatter.4
  309.7 31.2 reduce-scatter.6
  534.6 31.2 reduce-scatter.8
  764.8 31.2 reduce-scatter.10
